TPU v7x, 256 devices: a whole 4x4x8 slice. The times are simulated.
256 devices in a mesh: dp: 8 (over z), ctx: 32 (over x, y, core).
Axes of the slice: x: 4, y: 4, z: 8, core: 2. Of those that a mesh axis runs over, the one named last changes fastest.
Arguments:
- queries: bfloat16 [8, 4096, 4096], P('dp', 'ctx'), may hold values from -120 to 120
- layer_input: bfloat16 [8, 4096, 4096], P('dp', 'ctx'), may hold values from -6 to 6
- key_value_weight: bfloat16 [4096, 1024], P(('dp', 'ctx')), may hold values from -0.25 to 0.25
- output_gradient: bfloat16 [8, 4096, 4096], P('dp', 'ctx'), may hold values from -6 to 6
- document_lengths: int32 [8, 32], P('dp'), may hold values from 1 to 1024, 4096 in all within a row
Outputs:
- attended: bfloat16 [8, 4096, 4096], P('dp', 'ctx')
- query_grad: bfloat16 [8, 4096, 4096], P('dp', 'ctx')
- input_grad: bfloat16 [8, 4096, 4096], P('dp', 'ctx')
Inputs may be any that keep to these rules, and one draw needn't show every extreme that they name: `document_lengths`: each row holds the lengths of the 32 documents of one sequence in order; they sum to 4096, and one of them is exactly 1024.
All inputs are finite; a program needn't handle non-finite values.
Results may differ from a plain program's by a relative error of at most 0.02.
The roundings to bfloat16 on the way count: a program that leaves them out, or rounds other values in their place, can miss the bound.
Values may be sent and summed in bfloat16 or wider, within the bound.
A program may use at most 128 MiB of HBM per device.

v0:
```python
import functools
import math

import jax
import jax.numpy as jnp
from jax import lax
from jax.experimental import pallas as pl
from jax.experimental.pallas import tpu as pltpu
from jax.sharding import PartitionSpec as P

QUERY_HEADS = 32
KEY_VALUE_HEADS = 4
HEAD_SIZE = 128
GROUP = QUERY_HEADS // KEY_VALUE_HEADS
NX, NY, NZ = 4, 4, 8
TOKENS = 128
PAIR = 2 * TOKENS
MODEL = 4096
HALF = MODEL // 2
SCALE = 1.0 / math.sqrt(HEAD_SIZE)
LOG2E = math.log2(math.e)
TOGETHER = 2
MESH = pl.DeviceIdType.MESH
F32 = jnp.float32
BF16 = jnp.bfloat16

SIZES = {"x": NX, "y": NY, "z": NZ}


def coordinates():
    z = lax.axis_index("dp")
    ctx = lax.axis_index("ctx")
    core = lax.rem(ctx, 2)
    y = lax.rem(ctx // 2, NY)
    x = ctx // (2 * NY)
    return x, y, z, core


def place(x, y, z, core):
    return (z, (x * NY + y) * 2 + core)


def neighbour(x, y, z, core, axis, step):
    size = SIZES[axis]
    if axis == "x":
        x = lax.rem(x + step + size, size)
    elif axis == "y":
        y = lax.rem(y + step + size, size)
    else:
        z = lax.rem(z + step + size, size)
    return place(x, y, z, core)


def entry_barrier(targets):
    barrier = pltpu.get_barrier_semaphore()
    for target in targets:
        pl.semaphore_signal(barrier, inc=1, device_id=target, device_id_type=MESH)
    pl.semaphore_wait(barrier, len(targets))


class Sends:
    def __init__(self, send_sem, recv_sem):
        self.send_sem, self.recv_sem, self.count = send_sem, recv_sem, 0

    def make(self, src, dst, device):
        index = self.count
        self.count += 1
        return pltpu.make_async_remote_copy(
            src_ref=src,
            dst_ref=dst,
            send_sem=self.send_sem.at[index],
            recv_sem=self.recv_sem.at[index],
            device_id=device,
            device_id_type=MESH,
        )


def fan(axis):
    size = SIZES[axis]
    return sorted(range(1 - size // 2, size // 2 + 1), key=abs)[1:]


def layer_kernel(
    lengths_ref, q_ref, g_ref, x_ref, w_ref,
    att_ref, dq_ref, ig_ref,
    wbuf, wother, xbuf, qsend, gsend, qh, gh, kv, bias, kt, vt, dkt, dvt, prob_ref, slope_ref,
    part, stage, land, flat, acc, atts, dqs, attr, dqr, igs, igr, send_sem, recv_sem, local_sem,
):
    coords = coordinates()
    x, y, z, core = coords
    other = 1 - core
    chip = x * NY + y
    partner = place(x, y, z, other)
    sends = Sends(send_sem, recv_sem)
    started = []

    def go(copy):
        copy.start()
        started.append(copy)
        return copy

    locals_count = [0]

    def local(src, dst):
        copy = pltpu.make_async_copy(src, dst, local_sem.at[locals_count[0]])
        locals_count[0] += 1
        copy.start()
        return copy

    def at(axis, step):
        return neighbour(*coords, axis, step)

    def index(axis, step):
        return lax.rem({"x": x, "y": y, "z": z}[axis] + step + SIZES[axis], SIZES[axis])

    mine = pl.ds(pl.multiple_of(core * TOKENS, TOKENS), TOKENS)
    yours = pl.ds(pl.multiple_of(other * TOKENS, TOKENS), TOKENS)
    ours = pl.ds(pl.multiple_of(core * HALF, HALF), HALF)
    theirs = pl.ds(pl.multiple_of(other * HALF, HALF), HALF)

    loads = [
        local(x_ref, xbuf.at[mine]),
        local(q_ref.at[:, theirs], qsend),
        local(g_ref.at[:, theirs], gsend),
        local(q_ref.at[:, ours], qh.at[mine]),
        local(g_ref.at[:, ours], gh.at[mine]),
    ]
    entry_barrier(
        [partner] + [at(axis, step) for axis in "xyz" for step in fan(axis)]
    )

    rows = pl.ds(pl.multiple_of(core * 16, 16), 16)
    swaps = []
    for a in range(2):
        for b in range(2):
            target = wbuf.at[a, z, x, y, rows, pl.ds(b * 128, 128)]
            away = pl.multiple_of(b * 512 + other * 256 + a * 128, 128)
            here = pl.multiple_of(b * 512 + core * 256 + a * 128, 128)
            swaps.append(go(sends.make(w_ref.at[:, pl.ds(away, 128)], target, partner)))
            target[...] = w_ref[:, pl.ds(here, 128)]
    for copy in swaps:
        copy.wait_recv()

    zfan = [
        go(sends.make(wbuf.at[0, z, x, y], wbuf.at[0, z, x, y], at("z", step)))
        for step in fan("z")
    ]
    yfan = [
        go(sends.make(wbuf.at[1, z, x, y], wbuf.at[1, z, x, y], at("y", step)))
        for step in fan("y")
    ]
    for copy in loads[:3]:
        copy.wait()
    swapx = go(sends.make(xbuf.at[mine], xbuf.at[mine], partner))
    swapq = go(sends.make(qsend, qh.at[mine], partner))
    swapg = go(sends.make(gsend, gh.at[mine], partner))
    for copy in yfan:
        copy.wait_recv()
    xfan = [
        go(sends.make(wbuf.at[1, z, x], wbuf.at[1, z, x], at("x", step)))
        for step in fan("x")
    ]
    for copy in zfan:
        copy.wait_recv()

    def keys_of(i, j):
        return wbuf.at[0, :, i, j, :, pl.ds(0, 128)]

    def values_of(i, j):
        return wbuf.at[0, :, i, j, :, pl.ds(128, 128)]

    first, second = [], []
    for step in fan("y"):
        first.append(
            (
                go(sends.make(keys_of(x, y), keys_of(x, y), at("y", step))),
                go(sends.make(values_of(x, y), values_of(x, y), at("x", step))),
            )
        )

    def onward(step):
        j, i = index("y", -step), index("x", -step)
        for to in fan("x"):
            second.append(go(sends.make(keys_of(x, j), keys_of(x, j), at("x", to))))
            second.append(go(sends.make(values_of(i, y), values_of(i, y), at("y", to))))

    onward(0)
    for step, (one, two) in zip(fan("y"), first):
        one.wait_recv()
        two.wait_recv()
        onward(step)
    for copy in xfan:
        copy.wait_recv()

    ring = []

    def round_z(step):
        copies = []
        for piece in range(2):
            half = pl.ds(piece * 2, 2)
            back = wbuf.at[1, index("z", 1 - step), half]
            ahead = wbuf.at[1, index("z", step - 1), half]
            if ring:
                for copy in ring[-1][2 * piece : 2 * piece + 2]:
                    copy.wait_recv()
            if step < NZ // 2 or piece == 0:
                copies.append(go(sends.make(back, back, at("z", 1))))
            if step < NZ // 2 or piece == 1:
                copies.append(go(sends.make(ahead, ahead, at("z", -1))))
        ring.append(copies)

    round_z(1)
    for copy in second:
        copy.wait_recv()
    swapx.wait_recv()

    def project(a):
        def body(k, total):
            columns = pl.ds(pl.multiple_of(k * 512, 512), 512)
            return total + jnp.dot(
                xbuf[:, columns], wbuf[a, k].reshape(512, 256), preferred_element_type=F32
            )
        total = lax.fori_loop(0, NZ, body, jnp.zeros((PAIR, 256), F32))
        for b in range(2):
            kv[2 * a + b, 4] = total[:, b * 128 : (b + 1) * 128].astype(BF16)

    def pass_on(a):
        hops, near, far = [], [], []
        for p in (2 * a, 2 * a + 1):
            hops.append(go(sends.make(kv.at[p, 4], kv.at[p, 0], at("x", 1))))
            for k in (1, 2, 3):
                near.append(sends.make(kv.at[p, 4], kv.at[p, 4 - k], at("y", k)))
                sends.count -= 1
                far.append(sends.make(kv.at[p, 0], kv.at[p, 4 - k], at("y", k)))

                @pl.when(y + k < NY)
                def _(copy=near[-1]):
                    copy.start()

                started.append(near[-1])
        half = pl.ds(pl.multiple_of(other * 4, 4), 4)
        whole = go(sends.make(wbuf.at[a, half], wother.at[a], partner))
        return hops, near, far, whole

    def pass_far(passed):
        hops, near, far, whole = passed
        for n, hop in enumerate(hops):
            hop.wait_recv()
            for k in (1, 2, 3):

                @pl.when(y + k >= NY)
                def _(copy=far[3 * n + k - 1]):
                    copy.start()

    def passed_all(passed):
        for copy in passed[1]:
            copy.wait_recv()

    row = lax.broadcasted_iota(jnp.int32, (PAIR, PAIR), 0)
    col = lax.broadcasted_iota(jnp.int32, (PAIR, PAIR), 1)
    nt = (((1,), (1,)), ((), ()))

    project(0)
    passed = pass_on(0)

    position = chip * PAIR + lax.broadcasted_iota(jnp.int32, (1, PAIR), 1)
    end = jnp.int32(0)
    start = jnp.zeros((1, PAIR), jnp.int32)
    for n in range(lengths_ref.shape[1]):
        end = end + lengths_ref[0, n]
        start = jnp.where(position >= end, end, start)
    for s in range(4):
        base = chip * PAIR + row
        if s < 3:
            key = base - (3 - s) * PAIR
        else:
            key = jnp.where(row <= col, base, base - 4 * PAIR)
        bias[s] = jnp.where(key >= start, 0.0, -1e30)

    round_z(2)
    pass_far(passed)
    for copy in loads[3:]:
        copy.wait()
    swapq.wait_recv()
    swapg.wait_recv()
    passed_all(passed)

    def prepare(a):
        kt[...] = kv[2 * a].reshape(5 * PAIR, HEAD_SIZE).T
        vt[...] = kv[2 * a + 1].reshape(5 * PAIR, HEAD_SIZE).T
        dkt[...] = jnp.zeros_like(dkt)
        dvt[...] = jnp.zeros_like(dvt)

    upper = jnp.concatenate([row <= col] * TOGETHER, axis=1)

    def attend(a, step):
        columns = [
            pl.ds(
                pl.multiple_of((a * GROUP + step * TOGETHER + n) * HEAD_SIZE, HEAD_SIZE),
                HEAD_SIZE,
            )
            for n in range(TOGETHER)
        ]
        q = jnp.concatenate([qh[:, c] for c in columns], axis=0)
        g = jnp.concatenate([gh[:, c] for c in columns], axis=0)
        gt = g.T
        keys = kv[2 * a].reshape(5 * PAIR, HEAD_SIZE)
        values = kv[2 * a + 1].reshape(5 * PAIR, HEAD_SIZE)

        def blocks(u, v):
            t = lax.dot_general(u, v, nt, preferred_element_type=F32)
            t = [t[s * PAIR : (s + 1) * PAIR] for s in range(5)]
            return [*t[1:4], jnp.where(upper, t[4], t[0])]

        score = [
            t * (SCALE * LOG2E) + jnp.concatenate([bias[s]] * TOGETHER, axis=1)
            for s, t in enumerate(blocks(keys, q))
        ]
        top = functools.reduce(
            jnp.maximum, [jnp.max(t, axis=0, keepdims=True) for t in score]
        )
        weight = [jnp.exp2(t - top) for t in score]
        total = sum(jnp.sum(t, axis=0, keepdims=True) for t in weight)
        inverse = 1.0 / total

        def split(ref, parts):
            for s in range(3):
                ref[(s + 1) * PAIR : (s + 2) * PAIR] = parts[s].astype(BF16)
            ref[0:PAIR] = jnp.where(upper, 0.0, parts[3]).astype(BF16)
            ref[4 * PAIR : 5 * PAIR] = jnp.where(upper, parts[3], 0.0).astype(BF16)

        split(prob_ref, weight)
        mixed = jnp.dot(vt[...], prob_ref[...], preferred_element_type=F32)
        out = (mixed * inverse).astype(BF16).astype(F32)
        for n, c in enumerate(columns):
            atts[:, c] = out[:, n * PAIR : (n + 1) * PAIR].T.astype(BF16)
        product = jnp.sum(gt.astype(F32) * out, axis=0, keepdims=True)
        prob = [t * inverse for t in weight]
        split(slope_ref, [t * (r - product) for t, r in zip(prob, blocks(values, g))])
        split(prob_ref, prob)
        dq = jnp.dot(kt[...], slope_ref[...], preferred_element_type=F32) * SCALE
        for n, c in enumerate(columns):
            dqs[:, c] = dq[:, n * PAIR : (n + 1) * PAIR].T.astype(BF16)
        dkt[...] += lax.dot_general(q.T, slope_ref[...], nt, preferred_element_type=F32)
        dvt[...] += lax.dot_general(gt, prob_ref[...], nt, preferred_element_type=F32)

    def attend_two(a, first):
        lax.fori_loop(first, first + 2, lambda n, c: (attend(a, n), c)[1], 0)

    outs, keeps = [], []

    def finish(a):
        part[2 * a] = (dkt[...] * SCALE).T.reshape(5, PAIR, HEAD_SIZE)
        part[2 * a + 1] = dvt[...].T.reshape(5, PAIR, HEAD_SIZE)
        returns = []
        for p in (2 * a, 2 * a + 1):
            for k in (1, 2, 3):
                stage[p, k] = part[p, 4 - k].astype(BF16)
                returns.append(go(sends.make(stage.at[p, k], land.at[p, k], at("y", -k))))
        cols = pl.ds(a * HALF // 2, HALF // 2)
        for src, dst, ref in ((atts, attr, att_ref), (dqs, dqr, dq_ref)):
            outs.append(go(sends.make(src.at[yours, cols], dst.at[:, cols], partner)))
            place_cols = pl.ds(pl.multiple_of(core * HALF + a * HALF // 2, HALF // 2), HALF // 2)
            keeps.append(local(src.at[mine, cols], ref.at[:, place_cols]))
        return returns

    def collect(a, returns):
        ups = []
        for b in range(2):
            p = 2 * a + b
            before, own = part[p, 0], part[p, 4]
            for k in (1, 2, 3):
                returns[3 * b + k - 1].wait_recv()
                value = land[p, k].astype(F32)
                before = before + jnp.where(y + k >= NY, value, 0.0)
                own = own + jnp.where(y + k < NY, value, 0.0)
            stage[p, 0] = before.astype(BF16)
            part[p, 4] = own
            ups.append(go(sends.make(stage.at[p, 0], land.at[p, 0], at("x", -1))))
        return ups

    def settle(a, ups):
        crosses = []
        for b in range(2):
            p = 2 * a + b
            ups[b].wait_recv()
            cols = pl.ds(b * 128, 128)
            block = flat.at[core * 2 + a, :, cols]
            block[...] = (part[p, 4] + land[p, 0].astype(F32)).astype(BF16)
            crosses.append(go(sends.make(block, block, partner)))
        return crosses

    def multiply(a, n):
        total = lax.dot_general(
            flat[core * 2 + a], wbuf[a, core * 4 + n].reshape(512, 256), nt,
            preferred_element_type=F32,
        )
        return total + lax.dot_general(
            flat[other * 2 + a], wother[a, n].reshape(512, 256), nt,
            preferred_element_type=F32,
        )

    prepare(0)
    attend_two(0, 0)
    round_z(3)
    attend(0, 2)
    round_z(4)
    attend(0, 3)
    returns0 = finish(0)
    for copy in ring[-1]:
        copy.wait_recv()
    project(1)
    passed1 = pass_on(1)
    ups0 = collect(0, returns0)
    pass_far(passed1)
    crosses0 = settle(0, ups0)
    passed_all(passed1)
    prepare(1)
    attend_two(1, 0)
    for copy in crosses0:
        copy.wait_recv()
    passed[3].wait_recv()
    attend_two(1, 2)
    returns1 = finish(1)
    passed1[3].wait_recv()
    for n in range(4):
        acc[:, n * 512 : (n + 1) * 512] = multiply(0, n)
    ups1 = collect(1, returns1)
    for copy in settle(1, ups1):
        copy.wait_recv()
    sends_ig = []
    for n in range(4):
        cols = slice(n * 512, (n + 1) * 512)
        igs[:, cols] = (acc[:, cols] + multiply(1, n)).astype(BF16)
        sends_ig.append(
            go(sends.make(igs.at[yours, pl.ds(n * 512, 512)], igr.at[:, pl.ds(n * 512, 512)], partner))
        )
    keeps.append(local(igs.at[mine], ig_ref.at[:, ours]))
    for copy in outs:
        copy.wait_recv()
    keeps.append(local(attr, att_ref.at[:, theirs]))
    keeps.append(local(dqr, dq_ref.at[:, theirs]))
    for copy in sends_ig:
        copy.wait_recv()
    keeps.append(local(igr, ig_ref.at[:, theirs]))
    for copy in started:
        copy.wait_send()
    for copy in keeps:
        copy.wait()


def shards(queries, layer_input, key_value_weight, output_gradient, document_lengths):
    anywhere = pl.BlockSpec(memory_space=pl.ANY)
    shape = jax.ShapeDtypeStruct((TOKENS, MODEL), BF16)
    sems = pltpu.SemaphoreType.DMA
    window = 5 * PAIR
    wide = TOGETHER * PAIR
    att, dq, ig = pl.pallas_call(
        layer_kernel,
        out_shape=(shape,) * 3,
        in_specs=[
            pl.BlockSpec(memory_space=pltpu.SMEM),
            anywhere,
            anywhere,
            anywhere,
            pl.BlockSpec(memory_space=pltpu.VMEM),
        ],
        out_specs=[anywhere] * 3,
        scratch_shapes=[
            pltpu.VMEM((2, NZ, NX, NY, 32, 256), BF16),
            pltpu.VMEM((2, NZ // 2, NX, NY, 32, 256), BF16),
            pltpu.VMEM((PAIR, MODEL), BF16),
            pltpu.VMEM((TOKENS, HALF), BF16),
            pltpu.VMEM((TOKENS, HALF), BF16),
            pltpu.VMEM((PAIR, HALF), BF16),
            pltpu.VMEM((PAIR, HALF), BF16),
            pltpu.VMEM((4, 5, PAIR, HEAD_SIZE), BF16),
            pltpu.VMEM((4, PAIR, PAIR), F32),
            pltpu.VMEM((HEAD_SIZE, window), BF16),
            pltpu.VMEM((HEAD_SIZE, window), BF16),
            pltpu.VMEM((HEAD_SIZE, window), F32),
            pltpu.VMEM((HEAD_SIZE, window), F32),
            pltpu.VMEM((window, wide), BF16),
            pltpu.VMEM((window, wide), BF16),
            pltpu.VMEM((4, 5, PAIR, HEAD_SIZE), F32),
            pltpu.VMEM((4, 4, PAIR, HEAD_SIZE), BF16),
            pltpu.VMEM((4, 4, PAIR, HEAD_SIZE), BF16),
            pltpu.VMEM((4, PAIR, 256), BF16),
            pltpu.VMEM((PAIR, HALF), F32),
            pltpu.VMEM((PAIR, HALF), BF16),
            pltpu.VMEM((PAIR, HALF), BF16),
            pltpu.VMEM((TOKENS, HALF), BF16),
            pltpu.VMEM((TOKENS, HALF), BF16),
            pltpu.VMEM((PAIR, HALF), BF16),
            pltpu.VMEM((TOKENS, HALF), BF16),
            sems((160,)),
            sems((160,)),
            sems((24,)),
        ],
        compiler_params=pltpu.CompilerParams(
            collective_id=0, has_side_effects=True, vmem_limit_bytes=61 << 20
        ),
        name="layer",
    )(document_lengths, queries[0], output_gradient[0], layer_input[0], key_value_weight)
    return (att[None], dq[None], ig[None])


def solution(mesh):
    return jax.shard_map(
        shards,
        mesh=mesh,
        in_specs=(
            P("dp", "ctx", None),
            P("dp", "ctx", None),
            P(("dp", "ctx"), None),
            P("dp", "ctx", None),
            P("dp", None),
        ),
        out_specs=(P("dp", "ctx", None), P("dp", "ctx", None), P("dp", "ctx", None)),
        check_vma=False,
    )
```

profile of v0, /device:TPU:1, one launch (start us, length us, event | category | flops | bytes accessed | tf_op | source)
XLA Modules:
  0.0 112.2 jit_solution(15601766267776902811)
XLA Ops:
  0.6 106.6 %layer.1 = (bf16[128,4096]{1,0:T(8,128)(2,1)}, bf16[128,4096]{1,0:T(8,128)(2,1)}, bf16[128,4096]{1,0:T(8,128)(2,1)}) custom-call(s32[1,32]{1,0:T(1,128)} %lengths_ref.1, bf16[128,4096]{1,0:T(8,128)(2,1)} %bitcast.6, bf16[128,4096]{1,0:T(8,128)(2,1)} %bitcast.7, bf16[128,4096]{1,0:T(8,128)(2,1)} %bitcast.8, bf16[16,1024]{1,0:T(8,128)(2,1)} %w_ref.1), custom_call_target="tpu_custom_call" | custom-call | tf_op jit(solution)/shard_map/layer/pallas_call | solution.py:458
  107.3 0.0 copy-start.1
  107.3 2.4 %copy.11 = bf16[1,128,4096]{2,1,0:T(8,128)(2,1)} copy(bf16[1,128,4096]{2,1,0:T(8,128)(2,1)} %bitcast.11) | data formatting | bytes 2097152
  109.7 0.0 copy-done.1
  109.7 0.0 copy-start
  109.7 1.0 copy.12
  110.6 0.6 copy-done
  111.3 1.0 copy.13
Async XLA Ops:
  107.3 2.4 %copy-start.1 = (bf16[128,4096]{1,0:T(8,128)(2,1)S(1)}, bf16[128,4096]{1,0:T(8,128)(2,1)}, u32[]{:S(2)}) copy-start(bf16[128,4096]{1,0:T(8,128)(2,1)} %get-tuple-element.7) | copy-start | bytes 3145732
  109.7 1.6 %copy-start = (bf16[128,4096]{1,0:T(8,128)(2,1)S(1)}, bf16[128,4096]{1,0:T(8,128)(2,1)}, u32[]{:S(2)}) copy-start(bf16[128,4096]{1,0:T(8,128)(2,1)} %get-tuple-element.8) | copy-start | bytes 3145732
where the time goes:
time: 112 us
  Pallas kernels  107 us (96%)
  local copies, waits for them, and re-layouts  4.95 us (4%)
    pallas_call x1, Pallas kernels, shards(): pl.pallas_call(layer_kernel, out_shape=(shape,) * 3, in_specs=[pl.BlockSp...  107 us
    unnamed x7, local copies, waits for them, and re-layouts  4.95 us

commit v1 on v0

--- a/solution.py
+++ b/solution.py
@@ -210,7 +210,9 @@
         ring.append(copies)
 
     round_z(1)
-    for copy in second:
+    for n, copy in enumerate(second):
+        if n in (6, 18):
+            round_z(2 if n == 6 else 3)
         copy.wait_recv()
     swapx.wait_recv()
 
@@ -277,8 +279,8 @@
             key = jnp.where(row <= col, base, base - 4 * PAIR)
         bias[s] = jnp.where(key >= start, 0.0, -1e30)
 
-    round_z(2)
     pass_far(passed)
+    round_z(4)
     for copy in loads[3:]:
         copy.wait()
     swapq.wait_recv()
@@ -401,26 +403,26 @@
         )
 
     prepare(0)
-    attend_two(0, 0)
-    round_z(3)
+    attend(0, 0)
+    for copy in ring[-1]:
+        copy.wait_recv()
+    project(1)
+    passed1 = pass_on(1)
+    attend(0, 1)
     attend(0, 2)
-    round_z(4)
+    pass_far(passed1)
     attend(0, 3)
     returns0 = finish(0)
-    for copy in ring[-1]:
-        copy.wait_recv()
-    project(1)
-    passed1 = pass_on(1)
-    ups0 = collect(0, returns0)
-    pass_far(passed1)
-    crosses0 = settle(0, ups0)
     passed_all(passed1)
     prepare(1)
     attend_two(1, 0)
+    ups0 = collect(0, returns0)
+    attend(1, 2)
+    crosses0 = settle(0, ups0)
+    attend(1, 3)
     for copy in crosses0:
         copy.wait_recv()
     passed[3].wait_recv()
-    attend_two(1, 2)
     returns1 = finish(1)
     passed1[3].wait_recv()
     for n in range(4):

time: 112 us -> 101 us (0.902); the launches traced: 112 us -> 100 us
  Pallas kernels: 107 us -> 94.4 us
    pallas_call x1, Pallas kernels: 107 us -> 94.4 us  [shards(): pl.pallas_call(layer_kernel, out_shape=(shape,) * 3, in_specs=[pl.BlockSp...]
where the time goes in v1:
time: 101 us; the launch traced here: 100 us
  Pallas kernels  94.4 us (93%)
  local copies, waits for them, and re-layouts  4.95 us (5%)
    pallas_call x1, Pallas kernels, shards(): pl.pallas_call(layer_kernel, out_shape=(shape,) * 3, in_specs=[pl.BlockSp...  94.4 us
    unnamed x7, local copies, waits for them, and re-layouts  4.95 us

profile of v1, /device:TPU:1, one launch (start us, length us, event | category | flops | bytes accessed | tf_op | source)
XLA Modules:
  0.0 100.0 jit_solution(4669927494075234146)
XLA Ops:
  0.6 94.4 %layer.1 = (bf16[128,4096]{1,0:T(8,128)(2,1)}, bf16[128,4096]{1,0:T(8,128)(2,1)}, bf16[128,4096]{1,0:T(8,128)(2,1)}) custom-call(s32[1,32]{1,0:T(1,128)} %lengths_ref.1, bf16[128,4096]{1,0:T(8,128)(2,1)} %bitcast.6, bf16[128,4096]{1,0:T(8,128)(2,1)} %bitcast.7, bf16[128,4096]{1,0:T(8,128)(2,1)} %bitcast.8, bf16[16,1024]{1,0:T(8,128)(2,1)} %w_ref.1), custom_call_target="tpu_custom_call" | custom-call | tf_op jit(solution)/shard_map/layer/pallas_call | solution.py:460
  95.0 0.0 copy-start.1
  95.0 2.4 %copy.11 = bf16[1,128,4096]{2,1,0:T(8,128)(2,1)} copy(bf16[1,128,4096]{2,1,0:T(8,128)(2,1)} %bitcast.11) | data formatting | bytes 2097152
  97.4 0.0 copy-done.1
  97.4 0.0 copy-start
  97.4 1.0 copy.12
  98.4 0.6 copy-done
  99.0 1.0 copy.13
Async XLA Ops:
  95.0 2.4 %copy-start.1 = (bf16[128,4096]{1,0:T(8,128)(2,1)S(1)}, bf16[128,4096]{1,0:T(8,128)(2,1)}, u32[]{:S(2)}) copy-start(bf16[128,4096]{1,0:T(8,128)(2,1)} %get-tuple-element.7) | copy-start | bytes 3145732
  97.4 1.6 %copy-start = (bf16[128,4096]{1,0:T(8,128)(2,1)S(1)}, bf16[128,4096]{1,0:T(8,128)(2,1)}, u32[]{:S(2)}) copy-start(bf16[128,4096]{1,0:T(8,128)(2,1)} %get-tuple-element.8) | copy-start | bytes 3145732

commit v2 on v1

--- a/solution.py
+++ b/solution.py
@@ -84,7 +84,7 @@
     lengths_ref, q_ref, g_ref, x_ref, w_ref,
     att_ref, dq_ref, ig_ref,
     wbuf, wother, xbuf, qsend, gsend, qh, gh, kv, bias, kt, vt, dkt, dvt, prob_ref, slope_ref,
-    part, stage, land, flat, acc, atts, dqs, attr, dqr, igs, igr, send_sem, recv_sem, local_sem,
+    part, stage, land, flat, acc, atts, dqs, igs, send_sem, recv_sem, local_sem,
 ):
     coords = coordinates()
     x, y, z, core = coords
@@ -217,12 +217,9 @@
     swapx.wait_recv()
 
     def project(a):
-        def body(k, total):
-            columns = pl.ds(pl.multiple_of(k * 512, 512), 512)
-            return total + jnp.dot(
-                xbuf[:, columns], wbuf[a, k].reshape(512, 256), preferred_element_type=F32
-            )
-        total = lax.fori_loop(0, NZ, body, jnp.zeros((PAIR, 256), F32))
+        total = jnp.dot(
+            xbuf[...], wbuf[a].reshape(MODEL, 256), preferred_element_type=F32
+        )
         for b in range(2):
             kv[2 * a + b, 4] = total[:, b * 128 : (b + 1) * 128].astype(BF16)
 
@@ -254,8 +251,8 @@
                 def _(copy=far[3 * n + k - 1]):
                     copy.start()
 
-    def passed_all(passed):
-        for copy in passed[1]:
+    def passed_some(passed, b):
+        for copy in passed[1][3 * b : 3 * b + 3]:
             copy.wait_recv()
 
     row = lax.broadcasted_iota(jnp.int32, (PAIR, PAIR), 0)
@@ -285,17 +282,16 @@
         copy.wait()
     swapq.wait_recv()
     swapg.wait_recv()
-    passed_all(passed)
+    passed_some(passed, 0)
 
     def prepare(a):
         kt[...] = kv[2 * a].reshape(5 * PAIR, HEAD_SIZE).T
-        vt[...] = kv[2 * a + 1].reshape(5 * PAIR, HEAD_SIZE).T
         dkt[...] = jnp.zeros_like(dkt)
         dvt[...] = jnp.zeros_like(dvt)
 
     upper = jnp.concatenate([row <= col] * TOGETHER, axis=1)
 
-    def attend(a, step):
+    def attend(a, step, passed=None, leave=None):
         columns = [
             pl.ds(
                 pl.multiple_of((a * GROUP + step * TOGETHER + n) * HEAD_SIZE, HEAD_SIZE),
@@ -307,7 +303,6 @@
         g = jnp.concatenate([gh[:, c] for c in columns], axis=0)
         gt = g.T
         keys = kv[2 * a].reshape(5 * PAIR, HEAD_SIZE)
-        values = kv[2 * a + 1].reshape(5 * PAIR, HEAD_SIZE)
 
         def blocks(u, v):
             t = lax.dot_general(u, v, nt, preferred_element_type=F32)
@@ -332,58 +327,65 @@
             ref[4 * PAIR : 5 * PAIR] = jnp.where(upper, parts[3], 0.0).astype(BF16)
 
         split(prob_ref, weight)
+        if passed is not None:
+            passed_some(passed, 1)
+            vt[...] = kv[2 * a + 1].reshape(5 * PAIR, HEAD_SIZE).T
         mixed = jnp.dot(vt[...], prob_ref[...], preferred_element_type=F32)
         out = (mixed * inverse).astype(BF16).astype(F32)
         for n, c in enumerate(columns):
             atts[:, c] = out[:, n * PAIR : (n + 1) * PAIR].T.astype(BF16)
         product = jnp.sum(gt.astype(F32) * out, axis=0, keepdims=True)
         prob = [t * inverse for t in weight]
+        split(prob_ref, prob)
+        dvt[...] += lax.dot_general(gt, prob_ref[...], nt, preferred_element_type=F32)
+        if leave is not None:
+            leave(a, 1)
+        values = kv[2 * a + 1].reshape(5 * PAIR, HEAD_SIZE)
         split(slope_ref, [t * (r - product) for t, r in zip(prob, blocks(values, g))])
-        split(prob_ref, prob)
         dq = jnp.dot(kt[...], slope_ref[...], preferred_element_type=F32) * SCALE
         for n, c in enumerate(columns):
             dqs[:, c] = dq[:, n * PAIR : (n + 1) * PAIR].T.astype(BF16)
         dkt[...] += lax.dot_general(q.T, slope_ref[...], nt, preferred_element_type=F32)
-        dvt[...] += lax.dot_general(gt, prob_ref[...], nt, preferred_element_type=F32)
 
     def attend_two(a, first):
         lax.fori_loop(first, first + 2, lambda n, c: (attend(a, n), c)[1], 0)
 
     outs, keeps = [], []
+    returns = {}
+
+    def leave(a, b):
+        p = 2 * a + b
+        part[p] = (dvt[...] if b else dkt[...] * SCALE).T.reshape(5, PAIR, HEAD_SIZE)
+        for k in (1, 2, 3):
+            stage[p, k] = part[p, 4 - k].astype(BF16)
+            returns[p, k] = go(sends.make(stage.at[p, k], land.at[p, k], at("y", -k)))
 
     def finish(a):
-        part[2 * a] = (dkt[...] * SCALE).T.reshape(5, PAIR, HEAD_SIZE)
-        part[2 * a + 1] = dvt[...].T.reshape(5, PAIR, HEAD_SIZE)
-        returns = []
-        for p in (2 * a, 2 * a + 1):
-            for k in (1, 2, 3):
-                stage[p, k] = part[p, 4 - k].astype(BF16)
-                returns.append(go(sends.make(stage.at[p, k], land.at[p, k], at("y", -k))))
+        leave(a, 0)
         cols = pl.ds(a * HALF // 2, HALF // 2)
-        for src, dst, ref in ((atts, attr, att_ref), (dqs, dqr, dq_ref)):
-            outs.append(go(sends.make(src.at[yours, cols], dst.at[:, cols], partner)))
+        for src, ref in ((atts, att_ref), (dqs, dq_ref)):
             place_cols = pl.ds(pl.multiple_of(core * HALF + a * HALF // 2, HALF // 2), HALF // 2)
+            outs.append(go(sends.make(src.at[yours, cols], ref.at[:, place_cols], partner)))
             keeps.append(local(src.at[mine, cols], ref.at[:, place_cols]))
-        return returns
-
-    def collect(a, returns):
-        ups = []
-        for b in range(2):
+
+    def collect(a):
+        ups = {}
+        for b in (1, 0):
             p = 2 * a + b
             before, own = part[p, 0], part[p, 4]
             for k in (1, 2, 3):
-                returns[3 * b + k - 1].wait_recv()
+                returns[p, k].wait_recv()
                 value = land[p, k].astype(F32)
                 before = before + jnp.where(y + k >= NY, value, 0.0)
                 own = own + jnp.where(y + k < NY, value, 0.0)
             stage[p, 0] = before.astype(BF16)
             part[p, 4] = own
-            ups.append(go(sends.make(stage.at[p, 0], land.at[p, 0], at("x", -1))))
+            ups[b] = go(sends.make(stage.at[p, 0], land.at[p, 0], at("x", -1)))
         return ups
 
     def settle(a, ups):
         crosses = []
-        for b in range(2):
+        for b in (1, 0):
             p = 2 * a + b
             ups[b].wait_recv()
             cols = pl.ds(b * 128, 128)
@@ -403,7 +405,7 @@
         )
 
     prepare(0)
-    attend(0, 0)
+    attend(0, 0, passed)
     for copy in ring[-1]:
         copy.wait_recv()
     project(1)
@@ -411,40 +413,34 @@
     attend(0, 1)
     attend(0, 2)
     pass_far(passed1)
-    attend(0, 3)
-    returns0 = finish(0)
-    passed_all(passed1)
+    attend(0, 3, None, leave)
+    finish(0)
+    passed_some(passed1, 0)
     prepare(1)
-    attend_two(1, 0)
-    ups0 = collect(0, returns0)
+    attend(1, 0, passed1)
+    attend(1, 1)
+    ups0 = collect(0)
     attend(1, 2)
     crosses0 = settle(0, ups0)
-    attend(1, 3)
+    attend(1, 3, None, leave)
     for copy in crosses0:
         copy.wait_recv()
     passed[3].wait_recv()
-    returns1 = finish(1)
+    finish(1)
     passed1[3].wait_recv()
     for n in range(4):
         acc[:, n * 512 : (n + 1) * 512] = multiply(0, n)
-    ups1 = collect(1, returns1)
+    ups1 = collect(1)
     for copy in settle(1, ups1):
         copy.wait_recv()
-    sends_ig = []
     for n in range(4):
-        cols = slice(n * 512, (n + 1) * 512)
+        cols = pl.ds(n * 512, 512)
+        placed = pl.ds(pl.multiple_of(core * HALF + n * 512, 512), 512)
         igs[:, cols] = (acc[:, cols] + multiply(1, n)).astype(BF16)
-        sends_ig.append(
-            go(sends.make(igs.at[yours, pl.ds(n * 512, 512)], igr.at[:, pl.ds(n * 512, 512)], partner))
-        )
-    keeps.append(local(igs.at[mine], ig_ref.at[:, ours]))
+        outs.append(go(sends.make(igs.at[yours, cols], ig_ref.at[:, placed], partner)))
+        keeps.append(local(igs.at[mine, cols], ig_ref.at[:, placed]))
     for copy in outs:
         copy.wait_recv()
-    keeps.append(local(attr, att_ref.at[:, theirs]))
-    keeps.append(local(dqr, dq_ref.at[:, theirs]))
-    for copy in sends_ig:
-        copy.wait_recv()
-    keeps.append(local(igr, ig_ref.at[:, theirs]))
     for copy in started:
         copy.wait_send()
     for copy in keeps:
@@ -491,16 +487,13 @@
             pltpu.VMEM((PAIR, HALF), F32),
             pltpu.VMEM((PAIR, HALF), BF16),
             pltpu.VMEM((PAIR, HALF), BF16),
-            pltpu.VMEM((TOKENS, HALF), BF16),
-            pltpu.VMEM((TOKENS, HALF), BF16),
             pltpu.VMEM((PAIR, HALF), BF16),
-            pltpu.VMEM((TOKENS, HALF), BF16),
             sems((160,)),
             sems((160,)),
             sems((24,)),
         ],
         compiler_params=pltpu.CompilerParams(
-            collective_id=0, has_side_effects=True, vmem_limit_bytes=61 << 20
+            collective_id=0, has_side_effects=True, vmem_limit_bytes=50 << 20
         ),
         name="layer",
     )(document_lengths, queries[0], output_gradient[0], layer_input[0], key_value_weight)

time: 101 us -> 94.6 us (0.937)
  Pallas kernels: 94.4 us -> 89.2 us
    pallas_call x1, Pallas kernels: 94.4 us -> 89.2 us  [shards(): pl.pallas_call(layer_kernel, out_shape=(shape,) * 3, in_specs=[pl.BlockSp...]
where the time goes in v2:
time: 94.6 us; the launch traced here: 94.1 us
  Pallas kernels  89.2 us (94%)
  local copies, waits for them, and re-layouts  4.32 us (5%)
    pallas_call x1, Pallas kernels, shards(): pl.pallas_call(layer_kernel, out_shape=(shape,) * 3, in_specs=[pl.BlockSp...  89.2 us
    unnamed x7, local copies, waits for them, and re-layouts  4.32 us

profile of v2, /device:TPU:1, one launch (start us, length us, event | category | flops | bytes accessed | tf_op | source)
XLA Modules:
  0.0 94.1 jit_solution(13510453007715475905)
XLA Ops:
  0.6 0.0 copy-start.1
  0.6 0.6 copy-done.1
  1.3 0.0 copy-start
  1.3 0.8 copy-done
  2.0 89.2 %layer.1 = (bf16[128,4096]{1,0:T(8,128)(2,1)S(1)}, bf16[128,4096]{1,0:T(8,128)(2,1)S(1)}, bf16[128,4096]{1,0:T(8,128)(2,1)S(1)}) custom-call(s32[1,32]{1,0:T(1,128)S(1)} %copy-done.1, bf16[128,4096]{1,0:T(8,128)(2,1)} %bitcast.9, bf16[128,4096]{1,0:T(8,128)(2,1)} %bitcast.10, bf16[128,4096]{1,0:T(8,128)(2,1)} %bitcast.11, bf16[16,1024]{1,0:T(8,128)(2,1)S(1)} %copy-done), custom_call_target="tpu_custom_call" | custom-call | tf_op jit(solution)/shard_map/layer/pallas_call | solution.py:456
  91.2 1.0 %copy.11 = bf16[1,128,4096]{2,1,0:T(8,128)(2,1)} copy(bf16[1,128,4096]{2,1,0:T(8,128)(2,1)S(1)} %bitcast.8) | data formatting | bytes 2097152
  92.2 1.0 %copy.12 = bf16[1,128,4096]{2,1,0:T(8,128)(2,1)} copy(bf16[1,128,4096]{2,1,0:T(8,128)(2,1)S(1)} %bitcast.7) | data formatting | bytes 2097152
  93.2 1.0 %copy.13 = bf16[1,128,4096]{2,1,0:T(8,128)(2,1)} copy(bf16[1,128,4096]{2,1,0:T(8,128)(2,1)S(1)} %bitcast.6) | data formatting | bytes 2097152
Async XLA Ops:
  0.6 0.7 copy-start.1
  1.3 0.8 copy-start

commit v3 on v2

--- a/solution.py
+++ b/solution.py
@@ -77,7 +77,7 @@
 
 def fan(axis):
     size = SIZES[axis]
-    return sorted(range(1 - size // 2, size // 2 + 1), key=abs)[1:]
+    return sorted(range(1 - size // 2, size // 2 + 1), key=abs)[:0:-1]
 
 
 def layer_kernel(
@@ -394,14 +394,10 @@
             crosses.append(go(sends.make(block, block, partner)))
         return crosses
 
-    def multiply(a, n):
-        total = lax.dot_general(
-            flat[core * 2 + a], wbuf[a, core * 4 + n].reshape(512, 256), nt,
-            preferred_element_type=F32,
-        )
-        return total + lax.dot_general(
-            flat[other * 2 + a], wother[a, n].reshape(512, 256), nt,
-            preferred_element_type=F32,
+    def multiply(a, n, side):
+        right = wbuf[a, core * 4 + n] if side is core else wother[a, n]
+        return lax.dot_general(
+            flat[side * 2 + a], right.reshape(512, 256), nt, preferred_element_type=F32
         )
 
     prepare(0)
@@ -429,14 +425,17 @@
     finish(1)
     passed1[3].wait_recv()
     for n in range(4):
-        acc[:, n * 512 : (n + 1) * 512] = multiply(0, n)
+        acc[:, n * 512 : (n + 1) * 512] = multiply(0, n, core) + multiply(0, n, other)
     ups1 = collect(1)
-    for copy in settle(1, ups1):
+    crosses1 = settle(1, ups1)
+    for n in range(4):
+        acc[:, n * 512 : (n + 1) * 512] += multiply(1, n, core)
+    for copy in crosses1:
         copy.wait_recv()
     for n in range(4):
         cols = pl.ds(n * 512, 512)
         placed = pl.ds(pl.multiple_of(core * HALF + n * 512, 512), 512)
-        igs[:, cols] = (acc[:, cols] + multiply(1, n)).astype(BF16)
+        igs[:, cols] = (acc[:, cols] + multiply(1, n, other)).astype(BF16)
         outs.append(go(sends.make(igs.at[yours, cols], ig_ref.at[:, placed], partner)))
         keeps.append(local(igs.at[mine, cols], ig_ref.at[:, placed]))
     for copy in outs:

time: 94.6 us -> 93.3 us (0.986)
  Pallas kernels: 89.2 us -> 87.5 us
    pallas_call x1, Pallas kernels: 89.2 us -> 87.5 us  [shards(): pl.pallas_call(layer_kernel, out_shape=(shape,) * 3, in_specs=[pl.BlockSp...]
where the time goes in v3:
time: 93.3 us; the launch traced here: 92.5 us
  Pallas kernels  87.5 us (94%)
  local copies, waits for them, and re-layouts  4.32 us (5%)
    pallas_call x1, Pallas kernels, shards(): pl.pallas_call(layer_kernel, out_shape=(shape,) * 3, in_specs=[pl.BlockSp...  87.5 us
    unnamed x7, local copies, waits for them, and re-layouts  4.32 us

profile of v3, /device:TPU:1, one launch (start us, length us, event | category | flops | bytes accessed | tf_op | source)
XLA Modules:
  0.0 92.5 jit_solution(13388514548167963983)
XLA Ops:
  0.6 0.0 copy-start.1
  0.6 0.6 copy-done.1
  1.3 0.0 copy-start
  1.3 0.8 copy-done
  2.0 87.5 %layer.1 = (bf16[128,4096]{1,0:T(8,128)(2,1)S(1)}, bf16[128,4096]{1,0:T(8,128)(2,1)S(1)}, bf16[128,4096]{1,0:T(8,128)(2,1)S(1)}) custom-call(s32[1,32]{1,0:T(1,128)S(1)} %copy-done.1, bf16[128,4096]{1,0:T(8,128)(2,1)} %bitcast.9, bf16[128,4096]{1,0:T(8,128)(2,1)} %bitcast.10, bf16[128,4096]{1,0:T(8,128)(2,1)} %bitcast.11, bf16[16,1024]{1,0:T(8,128)(2,1)S(1)} %copy-done), custom_call_target="tpu_custom_call" | custom-call | tf_op jit(solution)/shard_map/layer/pallas_call | solution.py:455
  89.6 1.0 %copy.11 = bf16[1,128,4096]{2,1,0:T(8,128)(2,1)} copy(bf16[1,128,4096]{2,1,0:T(8,128)(2,1)S(1)} %bitcast.8) | data formatting | bytes 2097152
  90.6 1.0 %copy.12 = bf16[1,128,4096]{2,1,0:T(8,128)(2,1)} copy(bf16[1,128,4096]{2,1,0:T(8,128)(2,1)S(1)} %bitcast.7) | data formatting | bytes 2097152
  91.5 1.0 %copy.13 = bf16[1,128,4096]{2,1,0:T(8,128)(2,1)} copy(bf16[1,128,4096]{2,1,0:T(8,128)(2,1)S(1)} %bitcast.6) | data formatting | bytes 2097152
Async XLA Ops:
  0.6 0.7 copy-start.1
  1.3 0.8 copy-start
